TPU v7x, 256 devices: a whole 4x4x8 slice. The times are simulated.
256 devices in a mesh: band: 8 (over z), rows: 32 (over x, y, core).
Axes of the slice: x: 4, y: 4, z: 8, core: 2. Of those that a mesh axis runs over, the one named last changes fastest.
Arguments:
- tiles: bfloat16 [32, 8, 4, 512, 512], P('rows', 'band'), may hold values from -0.25 to 0.25
- tile_row: int32 [32, 8, 4], P('rows', 'band'), may hold values from 0 to 7
- tile_col: int32 [32, 8, 4], P('rows', 'band'), may hold values from 0 to 31
- tile_count: int32 [32, 8], P('rows', 'band'), may hold values from 1 to 4, as said below
- damping: float32 [128], replicated, may hold values from 0.5 to 2
- right_side: float32 [131072, 128], P(('rows', 'band')), may hold values from -40 to 40
Outputs:
- basis: float32 [4, 131072, 128], P(None, ('rows', 'band'))
- hessenberg: float32 [4, 3, 128], replicated
Inputs may be any that keep to these rules, and one draw needn't show every extreme that they name: `tile_count`: slots at or past the count hold tiles that are not part of the matrix; some row shard and band holds exactly 4 live tiles.
All inputs are finite; a program needn't handle non-finite values.
Results may differ from a plain program's by a relative error of at most 0.007.
Values may be sent and summed in bfloat16 or wider, within the bound.
A program may use at most 64 MiB of HBM per device.

v0:
```python
import math

import jax
import jax.numpy as jnp
from jax import lax
from jax.sharding import Mesh
from jax.sharding import PartitionSpec as P

ITERS = 3
ROWS_BAND = ("rows_0", "rows_1", "rows_2", "band")
ROWS = ("rows_0", "rows_1", "rows_2")


EPS = 1e-06


def sent_to_all(x, axis):
    count = lax.axis_size(axis)
    return lax.all_to_all(jnp.broadcast_to(x[None], (count, *x.shape)), axis, 0, 0, tiled=True)


def taken_together(x, axis):
    everything = sent_to_all(x, axis)
    return jnp.sum(everything, axis=0)


def by_axis(x, axes):
    far, near = axes
    return taken_together(taken_together(x, near), far)


def in_one(arrays, axis):
    flat, at, finished = (jnp.concatenate([a.reshape(-1) for a in arrays]), 0, [])
    subtotal = by_axis(flat, axis)
    for a in arrays:
        finished.append(subtotal[at : at + a.size].reshape(a.shape))
        at += a.size
    return tuple(finished)


def laid_out(pieces, dim):
    dims = list(pieces.shape[1:])
    dims[dim] *= pieces.shape[0]
    return jnp.moveaxis(pieces, 0, dim).reshape(dims)


def gather_axes(x, axes, dim):
    far, near = axes
    leading = sent_to_all(x, far)
    pieces = jnp.swapaxes(sent_to_all(leading, near), 0, 1)
    return laid_out(pieces.reshape(-1, *x.shape), dim)


def in_blocks(x, dim, count):
    dims = x.shape
    pieces = x.reshape(*dims[:dim], count, dims[dim] // count, *dims[dim + 1 :])
    return jnp.moveaxis(pieces, dim, 0)


def sent_and_summed(x, axis, dim):
    count = lax.axis_size(axis)
    pieces = lax.all_to_all(in_blocks(x, dim, count), axis, 0, 0, tiled=True)
    return jnp.sum(pieces.astype(jnp.float32), axis=0)


def global_sum(values):
    return in_one((values[0], values[1]), (("rows_0", "rows_1"), ("rows_2", "band")))


def multiply(local_tiles, tile_rows, tile_cols, live_count, column_block, bands):
    slot_count = local_tiles.shape[0]
    width = column_block.shape[1]
    queries = column_block.shape[2]
    picked = jnp.take(column_block, tile_cols, axis=0)
    products = jnp.einsum("sij,sjq->siq", local_tiles, picked, preferred_element_type=jnp.float32)
    live = jnp.arange(slot_count, dtype=jnp.int32) < live_count
    targets = jnp.arange(bands, dtype=jnp.int32)
    onehot = ((tile_rows[:, None] == targets[None, :]) & live[:, None]).astype(jnp.float32)
    partial_value = jnp.einsum("st,siq->tiq", onehot, products, precision=lax.Precision.HIGHEST)
    return partial_value.reshape(bands * width, queries)


def on_device(tiles, tile_row, tile_col, tile_count, damping, right_side):
    local_tiles = tiles[0, 0]
    tile_rows = tile_row[0, 0]
    tile_cols = tile_col[0, 0]
    live_count = tile_count[0, 0]
    bands = lax.axis_size("band")
    shards = lax.axis_size(ROWS)
    width = right_side.shape[0]
    queries = right_side.shape[1]
    rescale = math.sqrt(width * bands * shards)
    start = by_axis(
        jnp.sum(right_side * right_side, axis=0), (("rows_0", "rows_1"), ("rows_2", "band"))
    )
    inverse = lax.rsqrt(start + EPS)
    vectors = [right_side * inverse[None, :]]
    hessenberg = jnp.zeros((ITERS + 1, ITERS, queries), jnp.float32)
    for step in range(ITERS):
        current = vectors[step]
        gathered = gather_axes(current.astype(jnp.bfloat16), (("rows_0", "rows_1"), "rows_2"), 0)
        column_block = gathered.reshape(shards, width, queries)
        partial_value = multiply(local_tiles, tile_rows, tile_cols, live_count, column_block, bands)
        image = sent_and_summed(partial_value.astype(jnp.bfloat16), "band", 0)
        image = image + damping[None, :] * current
        stacked = jnp.stack(vectors[: step + 1])
        coefficients, squares_whole = global_sum(
            (jnp.sum(stacked * image[None], axis=1), jnp.sum(image * image, axis=0))
        )
        image = image - jnp.sum(coefficients[:, None, :] * stacked, axis=0)
        squares = squares_whole - jnp.sum(coefficients * coefficients, axis=0)
        hessenberg = hessenberg.at[: step + 1, step].set(coefficients)
        norm = jnp.sqrt(squares + EPS)
        hessenberg = hessenberg.at[step + 1, step].set(norm)
        vectors.append(image / norm[None, :])
    basis = jnp.stack([vector for vector in vectors]) * rescale
    return (basis, hessenberg)


def solution(mesh):
    finer = Mesh(
        mesh.devices.reshape(mesh.shape["band"], 4, 4, 2), ("band", "rows_0", "rows_1", "rows_2")
    )
    return jax.shard_map(
        on_device,
        mesh=finer,
        in_specs=(
            P(ROWS, "band", None, None, None),
            P(ROWS, "band", None),
            P(ROWS, "band", None),
            P(ROWS, "band"),
            P(),
            P(ROWS_BAND, None),
        ),
        out_specs=(P(None, ROWS_BAND, None), P()),
        check_vma=False,
    )
```

profile of v0, /device:TPU:1, one launch (start us, length us, event | category | flops | bytes accessed | tf_op | source)
XLA Modules:
  0.0 364.1 jit_solution(8866776312173580776)
XLA Ops:
  1.8 16.8 %all_to_all.93 = f32[16,1,128]{2,1,0:T(1,128)S(1)} all-to-all(f32[16,1,128]{2,1,0:T(1,128)S(1)} %broadcast_in_dim.37), channel_id=1, replica_groups=mesh['band'=8,'rows_0'=4,'rows_1'=4,'rows_2'=2] {'rows_2','band'}, dimensions={0} | all-to-all | bytes 16384 | tf_op jit(solution)/shard_map/all_to_all | solution.py:19
  18.6 13.0 %all_to_all.94 = f32[16,1,128]{2,1,0:T(1,128)S(1)} all-to-all(f32[16,1,128]{2,1,0:T(1,128)S(1)} %broadcast_in_dim.38), channel_id=1, replica_groups=mesh['band'=8,'rows_0'=4,'rows_1'=4,'rows_2'=2] {'rows_0','rows_1'}, dimensions={0} | all-to-all | bytes 16384 | tf_op jit(solution)/shard_map/all_to_all | solution.py:19
  34.3 4.6 %all-to-all-start.2 = ((bf16[16,512,128]{2,1,0:T(8,128)(2,1)}), bf16[16,512,128]{2,1,0:T(8,128)(2,1)}, u32[]{:S(2)}, u32[]{:S(2)}) async-start(bf16[16,512,128]{2,1,0:T(8,128)(2,1)} %broadcast_in_dim.39), calls=%async_computation.2 | async-start | bytes 4194304 | tf_op jit(solution)/shard_map/all_to_all | solution.py:19
  39.6 25.2 %all-to-all-done.2 = bf16[16,512,128]{2,1,0:T(8,128)(2,1)} async-done(((bf16[16,512,128]{2,1,0:T(8,128)(2,1)}), bf16[16,512,128]{2,1,0:T(8,128)(2,1)}, u32[]{:S(2)}, u32[]{:S(2)}) %all-to-all-start.2) | async-done | bytes 2097184 | tf_op jit(solution)/shard_map/all_to_all | solution.py:19
  64.8 2.5 broadcast_in_dim.40
  67.4 11.5 %all_to_all.95 = bf16[2,16,512,128]{3,2,1,0:T(8,128)(2,1)S(1)} all-to-all(bf16[2,16,512,128]{3,2,1,0:T(8,128)(2,1)S(1)} %broadcast_in_dim.40), channel_id=1, replica_groups=mesh['band'=8,'rows_0'=4,'rows_1'=4,'rows_2'=2] {'rows_2'}, dimensions={0} | all-to-all | bytes 8388608 | tf_op jit(solution)/shard_map/all_to_all | solution.py:19
  78.9 2.2 copy.38
  81.1 2.8 gather_fusion
  85.9 2.5 copy.40
  88.4 2.6 convolution_convert_fusion.2
  91.3 31.7 %all_to_all.96 = bf16[8,512,128]{2,1,0:T(8,128)(2,1)S(1)} all-to-all(bf16[8,512,128]{2,1,0:T(8,128)(2,1)S(1)} %copy.41), channel_id=1, replica_groups=mesh['band'=8,'rows_0'=4,'rows_1'=4,'rows_2'=2] {'band'}, dimensions={0} | all-to-all | bytes 2097152 | tf_op jit(solution)/shard_map/all_to_all | solution.py:62
  123.3 9.9 %all_to_all.97 = f32[16,1,256]{2,1,0:T(1,128)S(1)} all-to-all(f32[16,1,256]{2,1,0:T(1,128)S(1)} %broadcast_in_dim.41), channel_id=1, replica_groups=mesh['band'=8,'rows_0'=4,'rows_1'=4,'rows_2'=2] {'rows_2','band'}, dimensions={0} | all-to-all | bytes 32768 | tf_op jit(solution)/shard_map/all_to_all | solution.py:19
  133.2 9.7 %all_to_all.98 = f32[16,1,256]{2,1,0:T(1,128)S(1)} all-to-all(f32[16,1,256]{2,1,0:T(1,128)S(1)} %broadcast_in_dim.42), channel_id=1, replica_groups=mesh['band'=8,'rows_0'=4,'rows_1'=4,'rows_2'=2] {'rows_0','rows_1'}, dimensions={0} | all-to-all | bytes 32768 | tf_op jit(solution)/shard_map/all_to_all | solution.py:19
  143.4 29.3 %all_to_all.99 = bf16[16,512,128]{2,1,0:T(8,128)(2,1)S(1)} all-to-all(bf16[16,512,128]{2,1,0:T(8,128)(2,1)S(1)} %broadcast_in_dim.43), channel_id=1, replica_groups=mesh['band'=8,'rows_0'=4,'rows_1'=4,'rows_2'=2] {'rows_0','rows_1'}, dimensions={0} | all-to-all | bytes 4194304 | tf_op jit(solution)/shard_map/all_to_all | solution.py:19
  174.0 9.8 %all_to_all.100 = bf16[2,16,512,128]{3,2,1,0:T(8,128)(2,1)S(1)} all-to-all(bf16[2,16,512,128]{3,2,1,0:T(8,128)(2,1)S(1)} %broadcast_in_dim.44), channel_id=1, replica_groups=mesh['band'=8,'rows_0'=4,'rows_1'=4,'rows_2'=2] {'rows_2'}, dimensions={0} | all-to-all | bytes 8388608 | tf_op jit(solution)/shard_map/all_to_all | solution.py:19
  185.9 2.8 gather_fusion.1
  190.7 2.5 copy.46
  193.3 2.6 convolution_convert_fusion.1
  196.1 31.6 %all_to_all.101 = bf16[8,512,128]{2,1,0:T(8,128)(2,1)S(1)} all-to-all(bf16[8,512,128]{2,1,0:T(8,128)(2,1)S(1)} %copy.47), channel_id=1, replica_groups=mesh['band'=8,'rows_0'=4,'rows_1'=4,'rows_2'=2] {'band'}, dimensions={0} | all-to-all | bytes 2097152 | tf_op jit(solution)/shard_map/all_to_all | solution.py:62
  228.0 9.9 %all_to_all.102 = f32[16,1,384]{2,1,0:T(1,128)S(1)} all-to-all(f32[16,1,384]{2,1,0:T(1,128)S(1)} %broadcast_in_dim.45), channel_id=1, replica_groups=mesh['band'=8,'rows_0'=4,'rows_1'=4,'rows_2'=2] {'rows_2','band'}, dimensions={0} | all-to-all | bytes 49152 | tf_op jit(solution)/shard_map/all_to_all | solution.py:19
  238.0 9.6 %all_to_all.103 = f32[16,1,384]{2,1,0:T(1,128)S(1)} all-to-all(f32[16,1,384]{2,1,0:T(1,128)S(1)} %broadcast_in_dim.46), channel_id=1, replica_groups=mesh['band'=8,'rows_0'=4,'rows_1'=4,'rows_2'=2] {'rows_0','rows_1'}, dimensions={0} | all-to-all | bytes 49152 | tf_op jit(solution)/shard_map/all_to_all | solution.py:19
  248.1 29.3 %all_to_all.104 = bf16[16,512,128]{2,1,0:T(8,128)(2,1)S(1)} all-to-all(bf16[16,512,128]{2,1,0:T(8,128)(2,1)S(1)} %broadcast_in_dim.47), channel_id=1, replica_groups=mesh['band'=8,'rows_0'=4,'rows_1'=4,'rows_2'=2] {'rows_0','rows_1'}, dimensions={0} | all-to-all | bytes 4194304 | tf_op jit(solution)/shard_map/all_to_all | solution.py:19
  278.7 9.8 %all_to_all.105 = bf16[2,16,512,128]{3,2,1,0:T(8,128)(2,1)S(1)} all-to-all(bf16[2,16,512,128]{3,2,1,0:T(8,128)(2,1)S(1)} %broadcast_in_dim.48), channel_id=1, replica_groups=mesh['band'=8,'rows_0'=4,'rows_1'=4,'rows_2'=2] {'rows_2'}, dimensions={0} | all-to-all | bytes 8388608 | tf_op jit(solution)/shard_map/all_to_all | solution.py:19
  290.7 2.8 gather_fusion.2
  295.4 2.5 copy.52
  298.0 2.6 convolution_convert_fusion
  301.8 4.2 %all-to-all-start.14 = ((bf16[8,512,128]{2,1,0:T(8,128)(2,1)}), bf16[8,512,128]{2,1,0:T(8,128)(2,1)}, u32[]{:S(2)}, u32[]{:S(2)}) async-start(bf16[8,512,128]{2,1,0:T(8,128)(2,1)} %copy.53), calls=%async_computation.14 | async-start | bytes 2097152 | tf_op jit(solution)/shard_map/all_to_all | solution.py:62
  306.8 28.5 %all-to-all-done.14 = bf16[8,512,128]{2,1,0:T(8,128)(2,1)} async-done(((bf16[8,512,128]{2,1,0:T(8,128)(2,1)}), bf16[8,512,128]{2,1,0:T(8,128)(2,1)}, u32[]{:S(2)}, u32[]{:S(2)}) %all-to-all-start.14) | async-done | bytes 1048608 | tf_op jit(solution)/shard_map/all_to_all | solution.py:62
  337.5 3.8 %all-to-all-start.15 = ((f32[16,1,512]{2,1,0:T(1,128)}), f32[16,1,512]{2,1,0:T(1,128)S(1)}, u32[]{:S(2)}, u32[]{:S(2)}) async-start(f32[16,1,512]{2,1,0:T(1,128)} %broadcast_in_dim.49), calls=%async_computation.15 | async-start | bytes 65536 | tf_op jit(solution)/shard_map/all_to_all | solution.py:19
  342.0 6.3 %all-to-all-done.15 = f32[16,1,512]{2,1,0:T(1,128)S(1)} async-done(((f32[16,1,512]{2,1,0:T(1,128)}), f32[16,1,512]{2,1,0:T(1,128)S(1)}, u32[]{:S(2)}, u32[]{:S(2)}) %all-to-all-start.15) | async-done | bytes 32800 | tf_op jit(solution)/shard_map/all_to_all | solution.py:19
  349.0 3.5 all-to-all-start.16
  354.5 4.4 %all-to-all-done.16 = f32[16,1,512]{2,1,0:T(1,128)S(1)} async-done(((f32[16,1,512]{2,1,0:T(1,128)}), f32[16,1,512]{2,1,0:T(1,128)S(1)}, u32[]{:S(2)}, u32[]{:S(2)}) %all-to-all-start.16) | async-done | bytes 32800 | tf_op jit(solution)/shard_map/all_to_all | solution.py:19
  (86 shorter events, 31.3 us)
Async XLA Ops:
  0.6 83.3 %copy-start = (bf16[1,1,4,512,512]{4,3,2,1,0:T(8,128)(2,1)S(1)}, bf16[1,1,4,512,512]{4,3,2,1,0:T(8,128)(2,1)}, u32[]{:S(2)}) copy-start(bf16[1,1,4,512,512]{4,3,2,1,0:T(8,128)(2,1)} %param.20) | copy-start | bytes 6291460
  34.3 5.2 %copy-start.5 = (s32[1,1,4]{2,1,0:T(1,128)S(1)}, s32[1,1,4]{2,1,0:T(1,128)}, u32[]{:S(2)}) copy-start(s32[1,1,4]{2,1,0:T(1,128)} %param.22) | copy-start | bytes 52
  34.3 30.5 %all-to-all-start.2 = ((bf16[16,512,128]{2,1,0:T(8,128)(2,1)}), bf16[16,512,128]{2,1,0:T(8,128)(2,1)}, u32[]{:S(2)}, u32[]{:S(2)}) async-start(bf16[16,512,128]{2,1,0:T(8,128)(2,1)} %broadcast_in_dim.39), calls=%async_computation.2 | async-start | bytes 4194304 | tf_op jit(solution)/shard_map/all_to_all | solution.py:19
  83.9 4.5 %copy-start.3 = (s32[1,1,4]{2,1,0:T(1,128)S(1)}, s32[1,1,4]{2,1,0:T(1,128)}, u32[]{:S(2)}) copy-start(s32[1,1,4]{2,1,0:T(1,128)} %param.21) | copy-start | bytes 52
  91.2 31.9 %copy-start.1 = (f32[512,128]{1,0:T(8,128)S(1)}, f32[512,128]{1,0:T(8,128)}, u32[]{:S(2)}) copy-start(f32[512,128]{1,0:T(8,128)} %param.25) | copy-start | bytes 786436
  91.3 31.9 %copy-start.2 = (f32[128]{0:T(128)S(1)}, f32[128]{0:T(128)}, u32[]{:S(2)}) copy-start(f32[128]{0:T(128)} %param.24) | copy-start | bytes 1540
  300.6 5.4 %copy-start.4 = (s32[3]{0:T(128)S(1)}, s32[3]{0:T(128)}, u32[]{:S(2)}) copy-start(s32[3]{0:T(128)} %constant.192.clone.1) | copy-start | bytes 40
  301.8 33.5 %all-to-all-start.14 = ((bf16[8,512,128]{2,1,0:T(8,128)(2,1)}), bf16[8,512,128]{2,1,0:T(8,128)(2,1)}, u32[]{:S(2)}, u32[]{:S(2)}) async-start(bf16[8,512,128]{2,1,0:T(8,128)(2,1)} %copy.53), calls=%async_computation.14 | async-start | bytes 2097152 | tf_op jit(solution)/shard_map/all_to_all | solution.py:62
  337.5 10.8 %all-to-all-start.15 = ((f32[16,1,512]{2,1,0:T(1,128)}), f32[16,1,512]{2,1,0:T(1,128)S(1)}, u32[]{:S(2)}, u32[]{:S(2)}) async-start(f32[16,1,512]{2,1,0:T(1,128)} %broadcast_in_dim.49), calls=%async_computation.15 | async-start | bytes 65536 | tf_op jit(solution)/shard_map/all_to_all | solution.py:19
  349.0 9.9 %all-to-all-start.16 = ((f32[16,1,512]{2,1,0:T(1,128)}), f32[16,1,512]{2,1,0:T(1,128)S(1)}, u32[]{:S(2)}, u32[]{:S(2)}) async-start(f32[16,1,512]{2,1,0:T(1,128)} %broadcast_in_dim.50), calls=%async_computation.16 | async-start | bytes 65536 | tf_op jit(solution)/shard_map/all_to_all | solution.py:19
where the time goes:
time: 365 us; the launch traced here: 364 us
  blocking collectives  222 us (61%)
  waiting for transfers between devices  64.5 us (18%)
  local copies, waits for them, and re-layouts  37.6 us (10%)
  starting transfers between devices  16.1 us (4%)
  matrix products  13.7 us (4%)
  other arithmetic  8.76 us (2%)
    all_to_all x11, blocking collectives, sent_to_all(): lax.all_to_all(jnp.broadcast_to(x[None], (count, *x.shape)), axis, 0, 0,...  159 us
    all_to_all x2, blocking collectives, sent_and_summed(): pieces = lax.all_to_all(in_blocks(x, dim, count), axis, 0, 0, tiled=True)  63.3 us
    all_to_all x3, waiting for transfers between devices, sent_to_all(): lax.all_to_all(jnp.broadcast_to(x[None], (count, *x.shape)), axis, 0, 0,...  36 us
    all_to_all x1, waiting for transfers between devices, sent_and_summed(): pieces = lax.all_to_all(in_blocks(x, dim, count), axis, 0, 0, tiled=True)  28.5 us
    all_to_all x3, starting transfers between devices, sent_to_all(): lax.all_to_all(jnp.broadcast_to(x[None], (count, *x.shape)), axis, 0, 0,...  11.9 us
    broadcast_in_dim x14, local copies, waits for them, and re-layouts, sent_to_all(): jnp.broadcast_to(x[None], (count, *x.shape))  8.77 us
    gather x3, local copies, waits for them, and re-layouts, multiply(): picked = jnp.take(column_block, tile_cols, axis=0)  8.5 us
    dot_general x3, matrix products, multiply(): jnp.einsum('st,siq->tiq', onehot, products, precision=lax.Precision.HIGHEST)  7.93 us
  transfers between devices with their start and end apart: 4, of which 4 were waited for; matrix products, arithmetic and copies ran while one was open for 1% of the time, Pallas kernels for 0%

commit v1 on v0

v1 whole, which is shorter than its diff:
```python
import functools
import math

import jax
import jax.numpy as jnp
from jax import lax
from jax.experimental import pallas as pl
from jax.experimental.pallas import tpu as pltpu
from jax.sharding import Mesh
from jax.sharding import PartitionSpec as P

EPS = 1e-06
ITERS = 3
SLOTS = 4
TILE = 512
QUERIES = 128
CHUNKS = 4
QC = QUERIES // CHUNKS
STAGGER = 2
NX, NY, NZ = 4, 4, 8
PLANE = NX * NY * 2


def wrap(value, count):
    return lax.rem(value + 2 * count, count)


def kernel(
    rescale,
    rows_ref, cols_ref, count_ref, damping_ref, right_ref, tiles_ref,
    basis_ref, hess_ref,
    *scratch,
):
    refs = list(scratch)
    gathered = [[refs.pop(0) for _ in range(CHUNKS)] for _ in range(ITERS)]
    sums_z = [[refs.pop(0) for _ in range(CHUNKS)] for _ in range(ITERS)]
    (tiles_in, tiles_t, right_v, vec, act, part, rs_send, damp_col, out_v, hess_v,
     ar_z, ar_x, ar_y, ar_c,
     in_sem, out_sem, ag_s, ag_r, rs_s, rs_r, ar_s, ar_r) = refs

    x, y, z, c = (lax.axis_index(name) for name in ("x", "y", "z", "c"))
    s = 1 - 2 * c

    tiles_copy = pltpu.make_async_copy(tiles_ref, tiles_in, in_sem.at[0])
    tiles_copy.start()
    right_copy = pltpu.make_async_copy(right_ref, right_v, in_sem.at[1])
    right_copy.start()

    barrier = pltpu.get_barrier_semaphore()
    peers = [{"z": wrap(z + k, NZ)} for k in range(1, NZ)]
    peers += [{"x": wrap(x + k, NX)} for k in range(1, NX)]
    peers += [{"y": wrap(y + k, NY)} for k in range(1, NY)]
    peers += [{"c": 1 - c}]
    for peer in peers:
        pl.semaphore_signal(barrier, inc=1, device_id=peer, device_id_type=pl.DeviceIdType.MESH)

    sent = []

    def send(src, dst, send_sem, recv_sem, peer):
        copy = pltpu.make_async_remote_copy(
            src_ref=src, dst_ref=dst, send_sem=send_sem, recv_sem=recv_sem,
            device_id=peer, device_id_type=pl.DeviceIdType.MESH,
        )
        copy.start()
        sent.append(copy)
        return copy

    right_copy.wait()
    for k in range(TILE // 128):
        vec[0, :, k * 128 : (k + 1) * 128] = right_v[k * 128 : (k + 1) * 128, :].T
    damp_row = damping_ref[...]
    lane = lax.broadcasted_iota(jnp.int32, (QC, 128), 1)
    sub = lax.broadcasted_iota(jnp.int32, (QC, 128), 0)
    hess_v[...] = jnp.zeros_like(hess_v)
    pl.semaphore_wait(barrier, len(peers))

    def setup():
        tiles_copy.wait()
        for slot in range(SLOTS):
            for k in range(TILE // 128):
                tiles_t[slot, :, k * 128 : (k + 1) * 128] = tiles_in[slot, k * 128 : (k + 1) * 128, :].T
            yield

    def chunk(ch):
        q0 = ch * QC
        qs = slice(q0, q0 + QC)
        eye = lane == sub + q0
        in_chunk = (lax.broadcasted_iota(jnp.int32, (1, 128), 1) // QC) == ch
        x_first = ch % 2 == 0
        first, second = ("x", "y") if x_first else ("y", "x")
        u, w = (x, y) if x_first else (y, x)

        def to_row(col):
            return jnp.sum(jnp.where(eye, col, 0.0), axis=0, keepdims=True)

        def to_col(row):
            return jnp.sum(jnp.where(eye, row, 0.0), axis=1, keepdims=True)

        def dot(a, b):
            return to_row(jnp.sum(a * b, axis=1, keepdims=True))

        def reduced(which, rows):
            result = []

            def run():
                filled = jnp.concatenate(
                    rows + [jnp.zeros((8 - len(rows), 128), jnp.float32)] * (len(rows) < 8), axis=0
                )
                stages = (("z", z, NZ, ar_z), ("x", x, NX, ar_x), ("y", y, NY, ar_y), ("c", c, 2, ar_c))
                total = filled
                for at, (axis, me, count, buf) in enumerate(stages):
                    here = buf.at[which, ch]
                    here[me] = total
                    copies = []
                    for k in range(1, count):
                        copies.append(send(
                            here.at[me], here.at[me], ar_s.at[which, ch, at, k - 1],
                            ar_r.at[which, ch, at, k - 1], {axis: wrap(me + k, count)},
                        ))
                    yield
                    for copy in copies:
                        copy.wait_recv()
                    total = here[0]
                    for k in range(1, count):
                        total = total + here[k]
                result.append(total)

            return run(), result

        gather = gathered[0][ch]
        own = c * 16 + w * 4 + u
        right = vec[0, qs, :]
        gather[own] = right.astype(jnp.bfloat16)
        summing, summed = reduced(0, [dot(right, right)])
        known = {}
        yield

        for step in range(ITERS):
            gather = gathered[step][ch]
            sem = lambda k: (ag_s.at[step, ch, k], ag_r.at[step, ch, k])
            row = lambda core, place: gather.at[pl.ds(core * 16 + place * 4, 4)]
            up = send(gather.at[own], gather.at[own], *sem(0), {first: wrap(u + s, 4)})
            down = send(gather.at[own], gather.at[own], *sem(1), {first: wrap(u - s, 4)})
            next(summing, None)
            yield
            up.wait_recv()
            behind = c * 16 + w * 4 + wrap(u - s, 4)
            relay = send(gather.at[behind], gather.at[behind], *sem(2), {first: wrap(u + s, 4)})
            next(summing, None)
            yield
            down.wait_recv()
            relay.wait_recv()
            mine = row(c, w)
            up = send(mine, mine, *sem(3), {second: wrap(w + s, 4)})
            down = send(mine, mine, *sem(4), {second: wrap(w - s, 4)})
            twin = [send(mine, mine, *sem(6), {"c": 1 - c})]
            next(summing, None)
            yield
            up.wait_recv()
            behind = row(c, wrap(w - s, 4))
            relay = send(behind, behind, *sem(5), {second: wrap(w + s, 4)})
            twin.append(send(behind, behind, *sem(7), {"c": 1 - c}))
            down.wait_recv()
            ahead = row(c, wrap(w + s, 4))
            twin.append(send(ahead, ahead, *sem(8), {"c": 1 - c}))
            next(summing, None)
            yield
            relay.wait_recv()
            across = row(c, wrap(w + 2, 4))
            twin.append(send(across, across, *sem(9), {"c": 1 - c}))
            next(summing, None)
            yield
            for copy in twin:
                copy.wait_recv()
            products = []
            for slot in range(SLOTS):
                col = cols_ref[slot]
                cx, cy, cc = col // 8, lax.rem(col // 2, 4), lax.rem(col, 2)
                place = cc * 16 + (cy * 4 + cx if x_first else cx * 4 + cy)
                products.append(jnp.dot(
                    gather[place], tiles_t[slot], preferred_element_type=jnp.float32
                ))
            for target in range(NZ):
                total = None
                for slot in range(SLOTS):
                    live = jnp.logical_and(rows_ref[slot] == target, slot < count_ref[0])
                    term = products[slot] * jnp.where(live, 1.0, 0.0)
                    total = term if total is None else total + term
                part[ch, target] = total

            arrive = sums_z[step][ch]

            def pass_on(k, value, direction):
                out = rs_send.at[step, ch, k]
                out[...] = value.astype(jnp.bfloat16)
                return send(
                    out, arrive.at[k], rs_s.at[step, ch, k], rs_r.at[step, ch, k],
                    {"z": wrap(z + direction, NZ)},
                )

            def mine_for(k):
                return part[ch, wrap(z + k * s, NZ)]

            fore = pass_on(0, mine_for(4), s)
            back = pass_on(4, mine_for(-3), -s)
            yield
            for k in range(1, 4):
                fore.wait_recv()
                fore = pass_on(k, mine_for(4 - k) + arrive[k - 1].astype(jnp.float32), s)
                if k < 3:
                    back.wait_recv()
                    back = pass_on(4 + k, mine_for(k - 3) + arrive[3 + k].astype(jnp.float32), -s)
                yield
            back.wait_recv()
            raw = part[ch, z] + arrive[6].astype(jnp.float32)
            fore.wait_recv()
            raw = raw + arrive[3].astype(jnp.float32)

            for _ in summing:
                pass
            g = summed[0]
            d = damp_row
            if step == 0:
                known["inv"] = lax.rsqrt(g[0:1] + EPS)
                inv = to_col(known["inv"])
                image = raw * inv
                v0 = vec[0, qs, :] * inv
                vec[0, qs, :] = v0
                act[0, qs, :] = image
                dots = [dot(v0, image), dot(image, image), dot(v0, v0)]
            elif step == 1:
                va, aa, vv = g[0:1], g[1:2], g[2:3]
                h00 = va + d * vv
                e = d - h00
                square = aa + 2.0 * e * va + e * e * vv
                h10 = jnp.sqrt(jnp.maximum(square, 0.0) + EPS)
                known.update(vv00=vv)
                store(0, 0, h00, in_chunk)
                store(1, 0, h10, in_chunk)
                e_col, h_col = to_col(e), to_col(1.0 / h10)
                v0, a0 = vec[0, qs, :], act[0, qs, :]
                v1 = (a0 + e_col * v0) * h_col
                image = (raw + e_col * a0) * h_col
                vec[1, qs, :] = v1
                act[1, qs, :] = image
                dots = [dot(v0, image), dot(v1, image), dot(image, image), dot(v0, v1), dot(v1, v1)]
            else:
                va0, va1, aa, v01, v11 = (g[k : k + 1] for k in range(5))
                v00 = known["vv00"]
                h01 = va0 + d * v01
                h11 = va1 + d * v11 - h01 * v01
                e = d - h11
                square = (
                    aa + e * e * v11 + h01 * h01 * v00
                    + 2.0 * e * va1 - 2.0 * h01 * va0 - 2.0 * e * h01 * v01
                )
                h21 = jnp.sqrt(jnp.maximum(square, 0.0) + EPS)
                known.update(v01=v01, v11=v11)
                store(0, 1, h01, in_chunk)
                store(1, 1, h11, in_chunk)
                store(2, 1, h21, in_chunk)
                e_col, f_col, h_col = to_col(e), to_col(h01), to_col(1.0 / h21)
                v0, v1 = vec[0, qs, :], vec[1, qs, :]
                a0, a1 = act[0, qs, :], act[1, qs, :]
                v2 = (a1 + e_col * v1 - f_col * v0) * h_col
                image = (raw + e_col * a1 - f_col * a0) * h_col
                vec[2, qs, :] = v2
                dots = [
                    dot(v0, image), dot(v1, image), dot(v2, image), dot(image, image),
                    dot(v0, v2), dot(v1, v2), dot(v2, v2),
                ]
            if step + 1 < ITERS:
                gathered[step + 1][ch][own] = image.astype(jnp.bfloat16)
            summing, summed = reduced(step + 1, dots)
            if step + 1 == ITERS:
                next(summing)
                yield
                for _ in summing:
                    yield

        va0, va1, va2, aa, v02, v12, v22 = (summed[0][k : k + 1] for k in range(7))
        v00, v01, v11 = known["vv00"], known["v01"], known["v11"]
        d = damp_row
        h02 = va0 + d * v02
        h12 = va1 + d * v12 - h02 * v01
        h22 = va2 + d * v22 - h02 * v02 - h12 * v12
        e = d - h22
        square = (
            aa + e * e * v22 + h02 * h02 * v00 + h12 * h12 * v11
            + 2.0 * (e * va2 - h02 * va0 - h12 * va1 - e * h02 * v02 - e * h12 * v12 + h02 * h12 * v01)
        )
        h32 = jnp.sqrt(jnp.maximum(square, 0.0) + EPS)
        store(0, 2, h02, in_chunk)
        store(1, 2, h12, in_chunk)
        store(2, 2, h22, in_chunk)
        store(3, 2, h32, in_chunk)
        e_col, f_col, k_col, h_col = to_col(e), to_col(h02), to_col(h12), to_col(1.0 / h32)
        vec[3, qs, :] = (image + e_col * vec[2, qs, :] - f_col * vec[0, qs, :] - k_col * vec[1, qs, :]) * h_col

    def store(i, j, row, mask):
        at = i * ITERS + j
        hess_v[at : at + 1, :] = jnp.where(mask, row, hess_v[at : at + 1, :])

    outs = []

    def emit(i):
        for k in range(TILE // 128):
            out_v[i, k * 128 : (k + 1) * 128, :] = vec[i, :, k * 128 : (k + 1) * 128].T * rescale
        copy = pltpu.make_async_copy(out_v.at[i], basis_ref.at[i], out_sem.at[i])
        copy.start()
        outs.append(copy)

    live = {ch: chunk(ch) for ch in range(CHUNKS)}
    preparing = setup()
    tick = 0
    ticks = {ch: 0 for ch in range(CHUNKS)}
    emitted = 0
    while live:
        for ch in list(live):
            if tick >= ch * STAGGER:
                try:
                    next(live[ch])
                    ticks[ch] += 1
                except StopIteration:
                    del live[ch]
        next(preparing, None)
        tick += 1
        if emitted < ITERS and min(ticks.values()) > 1 + 9 * (emitted + 1):
            emit(emitted)
            emitted += 1
    while emitted < ITERS + 1:
        emit(emitted)
        emitted += 1
    hess_copy = pltpu.make_async_copy(hess_v, hess_ref, out_sem.at[ITERS + 1])
    hess_copy.start()
    for copy in sent:
        copy.wait_send()
    for copy in outs:
        copy.wait()
    hess_copy.wait()


def on_device(tiles, tile_row, tile_col, tile_count, damping, right_side):
    width, queries = right_side.shape
    rescale = math.sqrt(width * NX * NY * NZ * 2)
    smem = pl.BlockSpec(memory_space=pltpu.SMEM)
    vmem = pl.BlockSpec(memory_space=pltpu.VMEM)
    hbm = pl.BlockSpec(memory_space=pl.ANY)
    dma = pltpu.SemaphoreType.DMA
    bf16, f32 = jnp.bfloat16, jnp.float32
    basis, hessenberg = pl.pallas_call(
        functools.partial(kernel, rescale),
        out_shape=(
            jax.ShapeDtypeStruct((ITERS + 1, width, queries), f32),
            jax.ShapeDtypeStruct(((ITERS + 1) * ITERS, queries), f32),
        ),
        in_specs=[smem, smem, smem, vmem, hbm, hbm],
        out_specs=(hbm, hbm),
        scratch_shapes=[pltpu.VMEM((PLANE, QC, TILE), bf16) for _ in range(ITERS * CHUNKS)]
        + [pltpu.VMEM((7, QC, TILE), bf16) for _ in range(ITERS * CHUNKS)]
        + [
            pltpu.VMEM((SLOTS, TILE, TILE), bf16),
            pltpu.VMEM((SLOTS, TILE, TILE), bf16),
            pltpu.VMEM((TILE, QUERIES), f32),
            pltpu.VMEM((ITERS + 1, QUERIES, TILE), f32),
            pltpu.VMEM((ITERS, QUERIES, TILE), f32),
            pltpu.VMEM((CHUNKS, NZ, QC, TILE), f32),
            pltpu.VMEM((ITERS, CHUNKS, 7, QC, TILE), bf16),
            pltpu.VMEM((8, QUERIES), f32),
            pltpu.VMEM((ITERS + 1, TILE, QUERIES), f32),
            pltpu.VMEM(((ITERS + 1) * ITERS, QUERIES), f32),
            pltpu.VMEM((ITERS + 1, CHUNKS, NZ, 8, 128), f32),
            pltpu.VMEM((ITERS + 1, CHUNKS, NX, 8, 128), f32),
            pltpu.VMEM((ITERS + 1, CHUNKS, NY, 8, 128), f32),
            pltpu.VMEM((ITERS + 1, CHUNKS, 2, 8, 128), f32),
            dma((2,)),
            dma((ITERS + 2,)),
            dma((ITERS, CHUNKS, 10)),
            dma((ITERS, CHUNKS, 10)),
            dma((ITERS, CHUNKS, 7)),
            dma((ITERS, CHUNKS, 7)),
            dma((ITERS + 1, CHUNKS, 4, 7)),
            dma((ITERS + 1, CHUNKS, 4, 7)),
        ],
        compiler_params=pltpu.CompilerParams(
            collective_id=0, has_side_effects=True, vmem_limit_bytes=60 * 1024 * 1024
        ),
    )(
        tile_row.reshape(SLOTS), tile_col.reshape(SLOTS), tile_count.reshape(1),
        damping.reshape(1, queries), right_side, tiles.reshape(SLOTS, TILE, TILE),
    )
    return basis, hessenberg.reshape(ITERS + 1, ITERS, queries)


def solution(mesh):
    finer = Mesh(mesh.devices.reshape(NZ, NX, NY, 2), ("z", "x", "y", "c"))
    rows = ("x", "y", "c")
    return jax.shard_map(
        on_device,
        mesh=finer,
        in_specs=(
            P(rows, "z", None, None, None),
            P(rows, "z", None),
            P(rows, "z", None),
            P(rows, "z"),
            P(),
            P((*rows, "z"), None),
        ),
        out_specs=(P(None, (*rows, "z"), None), P()),
        check_vma=False,
    )
```

time: 365 us -> 174 us (0.48)
  blocking collectives: 222 us -> 0 us
  Pallas kernels: 0 us -> 169 us
  waiting for transfers between devices: 64.5 us -> 0 us
  local copies, waits for them, and re-layouts: 37.6 us -> 3.56 us
  starting transfers between devices: 16.1 us -> 0 us
  matrix products: 13.7 us -> 0 us
  other arithmetic: 8.76 us -> 0 us
    all_to_all x13 -> x0, blocking collectives: 222 us -> none  [the longest x11 159 us: sent_to_all(): lax.all_to_all(jnp.broadcast_to(x[None], (count, *x.shape)), axis, 0, 0,...]
    pallas_call x0 -> x1, Pallas kernels: none -> 169 us  [on_device(): pl.pallas_call(functools.partial(kernel, rescale), out_shape=(jax.ShapeDt...]
    all_to_all x4 -> x0, waiting for transfers between devices: 64.5 us -> none  [the longest x3 36 us: sent_to_all(): lax.all_to_all(jnp.broadcast_to(x[None], (count, *x.shape)), axis, 0, 0,...]
    all_to_all x4 -> x0, starting transfers between devices: 16.1 us -> none  [the longest x3 11.9 us: sent_to_all(): lax.all_to_all(jnp.broadcast_to(x[None], (count, *x.shape)), axis, 0, 0,...]
    dot_general x6 -> x0, matrix products: 13.7 us -> none  [the longest x3 7.93 us: multiply(): jnp.einsum('st,siq->tiq', onehot, products, precision=lax.Precision.HIGHEST)]
    broadcast_in_dim x14 -> x0, local copies, waits for them, and re-layouts: 8.77 us -> none  [sent_to_all(): jnp.broadcast_to(x[None], (count, *x.shape))]
    gather x3 -> x0, local copies, waits for them, and re-layouts: 8.5 us -> none  [multiply(): picked = jnp.take(column_block, tile_cols, axis=0)]
    dot_general x3 -> x0, local copies, waits for them, and re-layouts: 7.65 us -> none  [multiply(): jnp.einsum('sij,sjq->siq', local_tiles, picked, preferred_element_type=jn...]
  transfers between devices with their start and end apart: 4 -> 0, of which waited for: 4 -> 0; matrix products, arithmetic and copies ran while one was open for 1% -> 0% of each run, Pallas kernels for 0% -> 0%
where the time goes in v1:
time: 174 us
  Pallas kernels  169 us (97%)
  local copies, waits for them, and re-layouts  3.56 us (2%)
    pallas_call x1, Pallas kernels, on_device(): pl.pallas_call(functools.partial(kernel, rescale), out_shape=(jax.ShapeDt...  169 us

profile of v1, /device:TPU:1, one launch (start us, length us, event | category | flops | bytes accessed | tf_op | source)
XLA Modules:
  0.0 174.0 jit_solution(10526793325113230906)
XLA Ops:
  1.3 169.2 %shard_map.77 = (f32[4,512,128]{2,1,0:T(8,128)}, f32[12,128]{1,0:T(8,128)}) custom-call(s32[4]{0:T(128)} %bitcast.7, s32[4]{0:T(128)} %bitcast.8, s32[1]{0:T(128)} %bitcast.5.count_ref, f32[1,128]{1,0:T(1,128)} %bitcast.9, f32[512,128]{1,0:T(8,128)} %right_ref.1, bf16[4,512,512]{2,1,0:T(8,128)(2,1)} %bitcast.6), custom_call_target="tpu_custom_call" | custom-call | tf_op jit(solution)/shard_map/pallas_call | solution.py:351
  170.5 0.7 reshape.27
  171.2 0.6 copy.9
  171.8 2.3 %copy.12 = f32[4,512,128]{2,1,0:T(8,128)} copy(f32[4,512,128]{2,1,0:T(8,128)} %get-tuple-element.12) | data formatting | bytes 2097152

commit v2 on v1

--- a/solution.py
+++ b/solution.py
@@ -16,7 +16,10 @@
 QUERIES = 128
 CHUNKS = 4
 QC = QUERIES // CHUNKS
-STAGGER = 2
+GROUP = 4
+STAGGER = 0
+STEP_TICKS = 8
+SUM_TICKS = (1, 2, 5)
 NX, NY, NZ = 4, 4, 8
 PLANE = NX * NY * 2
 
@@ -35,7 +38,7 @@
     gathered = [[refs.pop(0) for _ in range(CHUNKS)] for _ in range(ITERS)]
     sums_z = [[refs.pop(0) for _ in range(CHUNKS)] for _ in range(ITERS)]
     (tiles_in, tiles_t, right_v, vec, act, part, rs_send, damp_col, out_v, hess_v,
-     ar_z, ar_x, ar_y, ar_c,
+     ar_z, ar_xy, ar_c,
      in_sem, out_sem, ag_s, ag_r, rs_s, rs_r, ar_s, ar_r) = refs
 
     x, y, z, c = (lax.axis_index(name) for name in ("x", "y", "z", "c"))
@@ -47,23 +50,38 @@
     right_copy.start()
 
     barrier = pltpu.get_barrier_semaphore()
-    peers = [{"z": wrap(z + k, NZ)} for k in range(1, NZ)]
-    peers += [{"x": wrap(x + k, NX)} for k in range(1, NX)]
-    peers += [{"y": wrap(y + k, NY)} for k in range(1, NY)]
-    peers += [{"c": 1 - c}]
+    across_z = [{"z": wrap(z + k, NZ)} for k in range(1, NZ)]
+    across_xy = [
+        {"x": wrap(x + i, NX), "y": wrap(y + k, NY)}
+        for i, k in ((2, 2), (1, 2), (3, 2), (2, 1), (2, 3), (1, 1), (3, 3), (1, 3), (3, 1),
+                     (2, 0), (0, 2), (1, 0), (3, 0), (0, 1), (0, 3))
+    ]
+    peers = across_z + across_xy + [{"c": 1 - c}]
     for peer in peers:
         pl.semaphore_signal(barrier, inc=1, device_id=peer, device_id_type=pl.DeviceIdType.MESH)
 
     sent = []
 
-    def send(src, dst, send_sem, recv_sem, peer):
-        copy = pltpu.make_async_remote_copy(
+    def remote(src, dst, send_sem, recv_sem, peer):
+        return pltpu.make_async_remote_copy(
             src_ref=src, dst_ref=dst, send_sem=send_sem, recv_sem=recv_sem,
             device_id=peer, device_id_type=pl.DeviceIdType.MESH,
         )
+
+    def send(*what):
+        remote(*what).start()
+
+    def send_one(*what):
+        copy = remote(*what)
         copy.start()
         sent.append(copy)
         return copy
+
+    def await_recv(size, send_sem, recv_sem):
+        remote(size, size, send_sem, recv_sem, {"c": 1 - c}).wait_recv()
+
+    def await_send(size, send_sem, recv_sem):
+        sent.append(remote(size, size, send_sem, recv_sem, {"c": 1 - c}))
 
     right_copy.wait()
     for k in range(TILE // 128):
@@ -81,7 +99,32 @@
                 tiles_t[slot, :, k * 128 : (k + 1) * 128] = tiles_in[slot, k * 128 : (k + 1) * 128, :].T
             yield
 
-    def chunk(ch):
+    def reduced(which, group, rows):
+        result = []
+
+        def run():
+            pad = [jnp.zeros((8 - len(rows), 128), jnp.float32)] if len(rows) < 8 else []
+            total = jnp.concatenate(rows + pad, axis=0)
+            stages = (
+                (c, [{"c": 1 - c}], ar_c), (z, across_z, ar_z), (x * NY + y, across_xy, ar_xy)
+            )
+            for at, (me, others, buf) in enumerate(stages):
+                here = buf.at[which, group]
+                here[me] = total
+                sems = ar_s.at[which, group, at], ar_r.at[which, group, at]
+                for peer in others:
+                    send(here.at[me], here.at[me], *sems, peer)
+                await_send(here.at[pl.ds(0, len(others))], *sems)
+                yield
+                await_recv(here.at[pl.ds(0, len(others))], *sems)
+                total = here[0]
+                for k in range(1, len(others) + 1):
+                    total = total + here[k]
+            result.append(total)
+
+        return run(), result
+
+    def chunk(ch, shared):
         q0 = ch * QC
         qs = slice(q0, q0 + QC)
         eye = lane == sub + q0
@@ -99,79 +142,47 @@
         def dot(a, b):
             return to_row(jnp.sum(a * b, axis=1, keepdims=True))
 
-        def reduced(which, rows):
-            result = []
-
-            def run():
-                filled = jnp.concatenate(
-                    rows + [jnp.zeros((8 - len(rows), 128), jnp.float32)] * (len(rows) < 8), axis=0
-                )
-                stages = (("z", z, NZ, ar_z), ("x", x, NX, ar_x), ("y", y, NY, ar_y), ("c", c, 2, ar_c))
-                total = filled
-                for at, (axis, me, count, buf) in enumerate(stages):
-                    here = buf.at[which, ch]
-                    here[me] = total
-                    copies = []
-                    for k in range(1, count):
-                        copies.append(send(
-                            here.at[me], here.at[me], ar_s.at[which, ch, at, k - 1],
-                            ar_r.at[which, ch, at, k - 1], {axis: wrap(me + k, count)},
-                        ))
-                    yield
-                    for copy in copies:
-                        copy.wait_recv()
-                    total = here[0]
-                    for k in range(1, count):
-                        total = total + here[k]
-                result.append(total)
-
-            return run(), result
-
         gather = gathered[0][ch]
         own = c * 16 + w * 4 + u
         right = vec[0, qs, :]
         gather[own] = right.astype(jnp.bfloat16)
-        summing, summed = reduced(0, [dot(right, right)])
+        shared["rows"].append([dot(right, right)])
         known = {}
-        yield
+
+        def row(core, place):
+            return gather.at[pl.ds(core * 16 + place * 4, 4)]
+
+        def pair(step, k):
+            return ag_s.at[step, ch, k], ag_r.at[step, ch, k]
 
         for step in range(ITERS):
             gather = gathered[step][ch]
-            sem = lambda k: (ag_s.at[step, ch, k], ag_r.at[step, ch, k])
-            row = lambda core, place: gather.at[pl.ds(core * 16 + place * 4, 4)]
-            up = send(gather.at[own], gather.at[own], *sem(0), {first: wrap(u + s, 4)})
-            down = send(gather.at[own], gather.at[own], *sem(1), {first: wrap(u - s, 4)})
-            next(summing, None)
-            yield
-            up.wait_recv()
-            behind = c * 16 + w * 4 + wrap(u - s, 4)
-            relay = send(gather.at[behind], gather.at[behind], *sem(2), {first: wrap(u + s, 4)})
-            next(summing, None)
-            yield
-            down.wait_recv()
-            relay.wait_recv()
+            early = pair(step, 0)
+            for k in (2, 1, 3):
+                send(gather.at[own], gather.at[own], *early, {first: wrap(u + k, 4)})
+            await_send(gather.at[pl.ds(0, 3)], *early)
+            yield
+            await_recv(gather.at[pl.ds(0, 3)], *early)
             mine = row(c, w)
-            up = send(mine, mine, *sem(3), {second: wrap(w + s, 4)})
-            down = send(mine, mine, *sem(4), {second: wrap(w - s, 4)})
-            twin = [send(mine, mine, *sem(6), {"c": 1 - c})]
-            next(summing, None)
+            up = send_one(mine, mine, *pair(step, 1), {second: wrap(w + s, 4)})
+            down = send_one(mine, mine, *pair(step, 2), {second: wrap(w - s, 4)})
+            twin = pair(step, 4)
+            send(mine, mine, *twin, {"c": 1 - c})
             yield
             up.wait_recv()
             behind = row(c, wrap(w - s, 4))
-            relay = send(behind, behind, *sem(5), {second: wrap(w + s, 4)})
-            twin.append(send(behind, behind, *sem(7), {"c": 1 - c}))
+            relay = send_one(behind, behind, *pair(step, 3), {second: wrap(w + s, 4)})
+            send(behind, behind, *twin, {"c": 1 - c})
             down.wait_recv()
             ahead = row(c, wrap(w + s, 4))
-            twin.append(send(ahead, ahead, *sem(8), {"c": 1 - c}))
-            next(summing, None)
+            send(ahead, ahead, *twin, {"c": 1 - c})
             yield
             relay.wait_recv()
-            across = row(c, wrap(w + 2, 4))
-            twin.append(send(across, across, *sem(9), {"c": 1 - c}))
-            next(summing, None)
-            yield
-            for copy in twin:
-                copy.wait_recv()
+            opposite = row(c, wrap(w + 2, 4))
+            send(opposite, opposite, *twin, {"c": 1 - c})
+            await_send(gather.at[pl.ds(0, 16)], *twin)
+            yield
+            await_recv(gather.at[pl.ds(0, 16)], *twin)
             products = []
             for slot in range(SLOTS):
                 col = cols_ref[slot]
@@ -193,7 +204,7 @@
             def pass_on(k, value, direction):
                 out = rs_send.at[step, ch, k]
                 out[...] = value.astype(jnp.bfloat16)
-                return send(
+                return send_one(
                     out, arrive.at[k], rs_s.at[step, ch, k], rs_r.at[step, ch, k],
                     {"z": wrap(z + direction, NZ)},
                 )
@@ -216,9 +227,7 @@
             fore.wait_recv()
             raw = raw + arrive[3].astype(jnp.float32)
 
-            for _ in summing:
-                pass
-            g = summed[0]
+            g = shared["total"]
             d = damp_row
             if step == 0:
                 known["inv"] = lax.rsqrt(g[0:1] + EPS)
@@ -271,14 +280,11 @@
                 ]
             if step + 1 < ITERS:
                 gathered[step + 1][ch][own] = image.astype(jnp.bfloat16)
-            summing, summed = reduced(step + 1, dots)
-            if step + 1 == ITERS:
-                next(summing)
-                yield
-                for _ in summing:
-                    yield
-
-        va0, va1, va2, aa, v02, v12, v22 = (summed[0][k : k + 1] for k in range(7))
+            shared["rows"].append(dots)
+        yield
+
+        g = shared["total"]
+        va0, va1, va2, aa, v02, v12, v22 = (g[k : k + 1] for k in range(7))
         v00, v01, v11 = known["vv00"], known["v01"], known["v11"]
         d = damp_row
         h02 = va0 + d * v02
@@ -298,8 +304,7 @@
         vec[3, qs, :] = (image + e_col * vec[2, qs, :] - f_col * vec[0, qs, :] - k_col * vec[1, qs, :]) * h_col
 
     def store(i, j, row, mask):
-        at = i * ITERS + j
-        hess_v[at : at + 1, :] = jnp.where(mask, row, hess_v[at : at + 1, :])
+        hess_v[i, j : j + 1, :] = jnp.where(mask, row, hess_v[i, j : j + 1, :])
 
     outs = []
 
@@ -310,22 +315,49 @@
         copy.start()
         outs.append(copy)
 
-    live = {ch: chunk(ch) for ch in range(CHUNKS)}
-    preparing = setup()
+    def together(group):
+        shared = {"rows": [], "total": None}
+        members = [chunk(group * GROUP + k, shared) for k in range(GROUP)]
+        for which in range(ITERS + 1):
+            for member in members:
+                next(member)
+            rows = [functools.reduce(jnp.add, same) for same in zip(*shared["rows"])]
+            shared["rows"] = []
+            summing, result = reduced(which, group, rows)
+            next(summing)
+            yield
+            if which < ITERS:
+                for tick in range(1, STEP_TICKS):
+                    if tick in SUM_TICKS:
+                        next(summing, None)
+                    for member in members:
+                        next(member)
+                    yield
+            for _ in summing:
+                if which == ITERS:
+                    yield
+            shared["total"] = result[0]
+        for member in members:
+            next(member, None)
+
+    groups = CHUNKS // GROUP
+    live = {group: together(group) for group in range(groups)}
+    ticks = [0] * groups
     tick = 0
-    ticks = {ch: 0 for ch in range(CHUNKS)}
     emitted = 0
     while live:
-        for ch in list(live):
-            if tick >= ch * STAGGER:
+        for group in list(live):
+            if tick >= group * STAGGER:
                 try:
-                    next(live[ch])
-                    ticks[ch] += 1
+                    next(live[group])
+                    ticks[group] += 1
                 except StopIteration:
-                    del live[ch]
-        next(preparing, None)
+                    del live[group]
+        if tick == 0:
+            for _ in setup():
+                pass
         tick += 1
-        if emitted < ITERS and min(ticks.values()) > 1 + 9 * (emitted + 1):
+        if emitted < ITERS and min(ticks) > STEP_TICKS * (emitted + 1):
             emit(emitted)
             emitted += 1
     while emitted < ITERS + 1:
@@ -352,7 +384,7 @@
         functools.partial(kernel, rescale),
         out_shape=(
             jax.ShapeDtypeStruct((ITERS + 1, width, queries), f32),
-            jax.ShapeDtypeStruct(((ITERS + 1) * ITERS, queries), f32),
+            jax.ShapeDtypeStruct((ITERS + 1, ITERS, queries), f32),
         ),
         in_specs=[smem, smem, smem, vmem, hbm, hbm],
         out_specs=(hbm, hbm),
@@ -368,19 +400,18 @@
             pltpu.VMEM((ITERS, CHUNKS, 7, QC, TILE), bf16),
             pltpu.VMEM((8, QUERIES), f32),
             pltpu.VMEM((ITERS + 1, TILE, QUERIES), f32),
-            pltpu.VMEM(((ITERS + 1) * ITERS, QUERIES), f32),
-            pltpu.VMEM((ITERS + 1, CHUNKS, NZ, 8, 128), f32),
-            pltpu.VMEM((ITERS + 1, CHUNKS, NX, 8, 128), f32),
-            pltpu.VMEM((ITERS + 1, CHUNKS, NY, 8, 128), f32),
-            pltpu.VMEM((ITERS + 1, CHUNKS, 2, 8, 128), f32),
+            pltpu.VMEM((ITERS + 1, ITERS, QUERIES), f32),
+            pltpu.VMEM((ITERS + 1, CHUNKS // GROUP, NZ, 8, 128), f32),
+            pltpu.VMEM((ITERS + 1, CHUNKS // GROUP, NX * NY, 8, 128), f32),
+            pltpu.VMEM((ITERS + 1, CHUNKS // GROUP, 2, 8, 128), f32),
             dma((2,)),
             dma((ITERS + 2,)),
-            dma((ITERS, CHUNKS, 10)),
-            dma((ITERS, CHUNKS, 10)),
+            dma((ITERS, CHUNKS, 5)),
+            dma((ITERS, CHUNKS, 5)),
             dma((ITERS, CHUNKS, 7)),
             dma((ITERS, CHUNKS, 7)),
-            dma((ITERS + 1, CHUNKS, 4, 7)),
-            dma((ITERS + 1, CHUNKS, 4, 7)),
+            dma((ITERS + 1, CHUNKS // GROUP, 3)),
+            dma((ITERS + 1, CHUNKS // GROUP, 3)),
         ],
         compiler_params=pltpu.CompilerParams(
             collective_id=0, has_side_effects=True, vmem_limit_bytes=60 * 1024 * 1024
@@ -389,7 +420,7 @@
         tile_row.reshape(SLOTS), tile_col.reshape(SLOTS), tile_count.reshape(1),
         damping.reshape(1, queries), right_side, tiles.reshape(SLOTS, TILE, TILE),
     )
-    return basis, hessenberg.reshape(ITERS + 1, ITERS, queries)
+    return basis, hessenberg
 
 
 def solution(mesh):

time: 174 us -> 122 us (0.70)
  Pallas kernels: 169 us -> 117 us
    pallas_call x1, Pallas kernels: 169 us -> 117 us  [on_device(): pl.pallas_call(functools.partial(kernel, rescale), out_shape=(jax.ShapeDt...]
where the time goes in v2:
time: 122 us
  Pallas kernels  117 us (96%)
  local copies, waits for them, and re-layouts  3.55 us (3%)
  between operations  1.29 us (1%)
    pallas_call x1, Pallas kernels, on_device(): pl.pallas_call(functools.partial(kernel, rescale), out_shape=(jax.ShapeDt...  117 us

profile of v2, /device:TPU:1, one launch (start us, length us, event | category | flops | bytes accessed | tf_op | source)
XLA Modules:
  0.0 121.9 jit_solution(4722437937982907819)
XLA Ops:
  1.3 117.1 %shard_map.77 = (f32[4,512,128]{2,1,0:T(8,128)}, f32[4,3,128]{2,1,0:T(4,128)}) custom-call(s32[4]{0:T(128)} %bitcast.7, s32[4]{0:T(128)} %bitcast.8, s32[1]{0:T(128)} %bitcast.5.count_ref, f32[1,128]{1,0:T(1,128)} %bitcast.9, f32[512,128]{1,0:T(8,128)} %right_ref.1, bf16[4,512,512]{2,1,0:T(8,128)(2,1)} %bitcast.6), custom_call_target="tpu_custom_call" | custom-call | tf_op jit(solution)/shard_map/pallas_call | solution.py:383
  118.4 1.3 %copy.8 = f32[4,3,128]{2,0,1:T(4,128)} copy(f32[4,3,128]{2,1,0:T(4,128)} %get-tuple-element.3) | data formatting | bytes 12288 | tf_op jit(solution)/shard_map/pallas_call | solution.py:383
  119.7 2.3 %copy.11 = f32[4,512,128]{2,1,0:T(8,128)} copy(f32[4,512,128]{2,1,0:T(8,128)} %get-tuple-element.6) | data formatting | bytes 2097152

commit v3 on v2

--- a/solution.py
+++ b/solution.py
@@ -19,7 +19,7 @@
 GROUP = 4
 STAGGER = 0
 STEP_TICKS = 8
-SUM_TICKS = (1, 2, 5)
+SUM_TICKS = (2,)
 NX, NY, NZ = 4, 4, 8
 PLANE = NX * NY * 2
 
@@ -38,7 +38,7 @@
     gathered = [[refs.pop(0) for _ in range(CHUNKS)] for _ in range(ITERS)]
     sums_z = [[refs.pop(0) for _ in range(CHUNKS)] for _ in range(ITERS)]
     (tiles_in, tiles_t, right_v, vec, act, part, rs_send, damp_col, out_v, hess_v,
-     ar_z, ar_xy, ar_c,
+     ar_zc, ar_xy,
      in_sem, out_sem, ag_s, ag_r, rs_s, rs_r, ar_s, ar_r) = refs
 
     x, y, z, c = (lax.axis_index(name) for name in ("x", "y", "z", "c"))
@@ -50,13 +50,15 @@
     right_copy.start()
 
     barrier = pltpu.get_barrier_semaphore()
-    across_z = [{"z": wrap(z + k, NZ)} for k in range(1, NZ)]
+    across_zc = [
+        {"z": wrap(z + k, NZ), "c": core} for k in (4, 3, 5, 2, 6, 1, 7) for core in (1 - c, c)
+    ] + [{"c": 1 - c}]
     across_xy = [
         {"x": wrap(x + i, NX), "y": wrap(y + k, NY)}
         for i, k in ((2, 2), (1, 2), (3, 2), (2, 1), (2, 3), (1, 1), (3, 3), (1, 3), (3, 1),
                      (2, 0), (0, 2), (1, 0), (3, 0), (0, 1), (0, 3))
     ]
-    peers = across_z + across_xy + [{"c": 1 - c}]
+    peers = across_zc + across_xy
     for peer in peers:
         pl.semaphore_signal(barrier, inc=1, device_id=peer, device_id_type=pl.DeviceIdType.MESH)
 
@@ -105,9 +107,7 @@
         def run():
             pad = [jnp.zeros((8 - len(rows), 128), jnp.float32)] if len(rows) < 8 else []
             total = jnp.concatenate(rows + pad, axis=0)
-            stages = (
-                (c, [{"c": 1 - c}], ar_c), (z, across_z, ar_z), (x * NY + y, across_xy, ar_xy)
-            )
+            stages = ((z * 2 + c, across_zc, ar_zc), (x * NY + y, across_xy, ar_xy))
             for at, (me, others, buf) in enumerate(stages):
                 here = buf.at[which, group]
                 here[me] = total
@@ -143,7 +143,7 @@
             return to_row(jnp.sum(a * b, axis=1, keepdims=True))
 
         gather = gathered[0][ch]
-        own = c * 16 + w * 4 + u
+        own = c * 16 + w * 4
         right = vec[0, qs, :]
         gather[own] = right.astype(jnp.bfloat16)
         shared["rows"].append([dot(right, right)])
@@ -157,27 +157,35 @@
 
         for step in range(ITERS):
             gather = gathered[step][ch]
-            early = pair(step, 0)
+            early, twin = pair(step, 0), pair(step, 4)
             for k in (2, 1, 3):
-                send(gather.at[own], gather.at[own], *early, {first: wrap(u + k, 4)})
+                send(gather.at[own], gather.at[own + 4 - k], *early, {first: wrap(u + k, 4)})
             await_send(gather.at[pl.ds(0, 3)], *early)
+
+            def spread(at, place, count, direction):
+                what = gather.at[pl.ds(place, count)]
+                return send_one(what, what, *pair(step, at), {second: wrap(w + direction, 4)})
+
+            up, down = spread(1, own, 1, s), spread(2, own, 1, -s)
             yield
             await_recv(gather.at[pl.ds(0, 3)], *early)
+            up_rest, down_rest = spread(5, own + 1, 3, s), spread(6, own + 1, 3, -s)
             mine = row(c, w)
-            up = send_one(mine, mine, *pair(step, 1), {second: wrap(w + s, 4)})
-            down = send_one(mine, mine, *pair(step, 2), {second: wrap(w - s, 4)})
-            twin = pair(step, 4)
             send(mine, mine, *twin, {"c": 1 - c})
-            yield
             up.wait_recv()
+            relay = spread(3, c * 16 + wrap(w - s, 4) * 4, 1, s)
+            yield
+            up_rest.wait_recv()
+            relay_rest = spread(7, c * 16 + wrap(w - s, 4) * 4 + 1, 3, s)
             behind = row(c, wrap(w - s, 4))
-            relay = send_one(behind, behind, *pair(step, 3), {second: wrap(w + s, 4)})
             send(behind, behind, *twin, {"c": 1 - c})
             down.wait_recv()
+            down_rest.wait_recv()
             ahead = row(c, wrap(w + s, 4))
             send(ahead, ahead, *twin, {"c": 1 - c})
             yield
             relay.wait_recv()
+            relay_rest.wait_recv()
             opposite = row(c, wrap(w + 2, 4))
             send(opposite, opposite, *twin, {"c": 1 - c})
             await_send(gather.at[pl.ds(0, 16)], *twin)
@@ -187,7 +195,8 @@
             for slot in range(SLOTS):
                 col = cols_ref[slot]
                 cx, cy, cc = col // 8, lax.rem(col // 2, 4), lax.rem(col, 2)
-                place = cc * 16 + (cy * 4 + cx if x_first else cx * 4 + cy)
+                cu, cw = (cx, cy) if x_first else (cy, cx)
+                place = cc * 16 + cw * 4 + lax.rem(cu - u + 4, 4)
                 products.append(jnp.dot(
                     gather[place], tiles_t[slot], preferred_element_type=jnp.float32
                 ))
@@ -401,17 +410,16 @@
             pltpu.VMEM((8, QUERIES), f32),
             pltpu.VMEM((ITERS + 1, TILE, QUERIES), f32),
             pltpu.VMEM((ITERS + 1, ITERS, QUERIES), f32),
-            pltpu.VMEM((ITERS + 1, CHUNKS // GROUP, NZ, 8, 128), f32),
+            pltpu.VMEM((ITERS + 1, CHUNKS // GROUP, NZ * 2, 8, 128), f32),
             pltpu.VMEM((ITERS + 1, CHUNKS // GROUP, NX * NY, 8, 128), f32),
-            pltpu.VMEM((ITERS + 1, CHUNKS // GROUP, 2, 8, 128), f32),
             dma((2,)),
             dma((ITERS + 2,)),
-            dma((ITERS, CHUNKS, 5)),
-            dma((ITERS, CHUNKS, 5)),
+            dma((ITERS, CHUNKS, 8)),
+            dma((ITERS, CHUNKS, 8)),
             dma((ITERS, CHUNKS, 7)),
             dma((ITERS, CHUNKS, 7)),
-            dma((ITERS + 1, CHUNKS // GROUP, 3)),
-            dma((ITERS + 1, CHUNKS // GROUP, 3)),
+            dma((ITERS + 1, CHUNKS // GROUP, 2)),
+            dma((ITERS + 1, CHUNKS // GROUP, 2)),
         ],
         compiler_params=pltpu.CompilerParams(
             collective_id=0, has_side_effects=True, vmem_limit_bytes=60 * 1024 * 1024

time: 122 us -> 118 us (0.967)
  Pallas kernels: 117 us -> 113 us
    pallas_call x1, Pallas kernels: 117 us -> 113 us  [on_device(): pl.pallas_call(functools.partial(kernel, rescale), out_shape=(jax.ShapeDt...]
where the time goes in v3:
time: 118 us
  Pallas kernels  113 us (96%)
  local copies, waits for them, and re-layouts  3.55 us (3%)
  between operations  1.29 us (1%)
    pallas_call x1, Pallas kernels, on_device(): pl.pallas_call(functools.partial(kernel, rescale), out_shape=(jax.ShapeDt...  113 us

profile of v3, /device:TPU:1, one launch (start us, length us, event | category | flops | bytes accessed | tf_op | source)
XLA Modules:
  0.0 118.1 jit_solution(3822099664306384433)
XLA Ops:
  1.3 113.2 %shard_map.77 = (f32[4,512,128]{2,1,0:T(8,128)}, f32[4,3,128]{2,1,0:T(4,128)}) custom-call(s32[4]{0:T(128)} %bitcast.7, s32[4]{0:T(128)} %bitcast.8, s32[1]{0:T(128)} %bitcast.5.count_ref, f32[1,128]{1,0:T(1,128)} %bitcast.9, f32[512,128]{1,0:T(8,128)} %right_ref.1, bf16[4,512,512]{2,1,0:T(8,128)(2,1)} %bitcast.6), custom_call_target="tpu_custom_call" | custom-call | tf_op jit(solution)/shard_map/pallas_call | solution.py:392
  114.5 1.3 %copy.8 = f32[4,3,128]{2,0,1:T(4,128)} copy(f32[4,3,128]{2,1,0:T(4,128)} %get-tuple-element.3) | data formatting | bytes 12288 | tf_op jit(solution)/shard_map/pallas_call | solution.py:392
  115.8 2.3 %copy.11 = f32[4,512,128]{2,1,0:T(8,128)} copy(f32[4,512,128]{2,1,0:T(8,128)} %get-tuple-element.6) | data formatting | bytes 2097152

commit v4 on v3

--- a/solution.py
+++ b/solution.py
@@ -19,7 +19,7 @@
 GROUP = 4
 STAGGER = 0
 STEP_TICKS = 8
-SUM_TICKS = (2,)
+SUM_TICKS = (2, 5)
 NX, NY, NZ = 4, 4, 8
 PLANE = NX * NY * 2
 
@@ -38,7 +38,7 @@
     gathered = [[refs.pop(0) for _ in range(CHUNKS)] for _ in range(ITERS)]
     sums_z = [[refs.pop(0) for _ in range(CHUNKS)] for _ in range(ITERS)]
     (tiles_in, tiles_t, right_v, vec, act, part, rs_send, damp_col, out_v, hess_v,
-     ar_zc, ar_xy,
+     ar_z, ar_c, ar_xy,
      in_sem, out_sem, ag_s, ag_r, rs_s, rs_r, ar_s, ar_r) = refs
 
     x, y, z, c = (lax.axis_index(name) for name in ("x", "y", "z", "c"))
@@ -50,15 +50,13 @@
     right_copy.start()
 
     barrier = pltpu.get_barrier_semaphore()
-    across_zc = [
-        {"z": wrap(z + k, NZ), "c": core} for k in (4, 3, 5, 2, 6, 1, 7) for core in (1 - c, c)
-    ] + [{"c": 1 - c}]
+    across_z = [{"z": wrap(z + k, NZ)} for k in (4, 3, 5, 2, 6, 1, 7)]
     across_xy = [
         {"x": wrap(x + i, NX), "y": wrap(y + k, NY)}
         for i, k in ((2, 2), (1, 2), (3, 2), (2, 1), (2, 3), (1, 1), (3, 3), (1, 3), (3, 1),
                      (2, 0), (0, 2), (1, 0), (3, 0), (0, 1), (0, 3))
     ]
-    peers = across_zc + across_xy
+    peers = across_z + across_xy + [{"c": 1 - c}]
     for peer in peers:
         pl.semaphore_signal(barrier, inc=1, device_id=peer, device_id_type=pl.DeviceIdType.MESH)
 
@@ -107,7 +105,7 @@
         def run():
             pad = [jnp.zeros((8 - len(rows), 128), jnp.float32)] if len(rows) < 8 else []
             total = jnp.concatenate(rows + pad, axis=0)
-            stages = ((z * 2 + c, across_zc, ar_zc), (x * NY + y, across_xy, ar_xy))
+            stages = ((c, [{"c": 1 - c}], ar_c), (z, across_z, ar_z), (x * NY + y, across_xy, ar_xy))
             for at, (me, others, buf) in enumerate(stages):
                 here = buf.at[which, group]
                 here[me] = total
@@ -146,7 +144,7 @@
         own = c * 16 + w * 4
         right = vec[0, qs, :]
         gather[own] = right.astype(jnp.bfloat16)
-        shared["rows"].append([dot(right, right)])
+        pending = [(right, right)]
         known = {}
 
         def row(core, place):
@@ -167,6 +165,7 @@
                 return send_one(what, what, *pair(step, at), {second: wrap(w + direction, 4)})
 
             up, down = spread(1, own, 1, s), spread(2, own, 1, -s)
+            shared["rows"].append([dot(*both) for both in pending])
             yield
             await_recv(gather.at[pl.ds(0, 3)], *early)
             up_rest, down_rest = spread(5, own + 1, 3, s), spread(6, own + 1, 3, -s)
@@ -200,13 +199,14 @@
                 products.append(jnp.dot(
                     gather[place], tiles_t[slot], preferred_element_type=jnp.float32
                 ))
-            for target in range(NZ):
+            def partial_sum(k):
+                target = wrap(z + k * s, NZ)
                 total = None
                 for slot in range(SLOTS):
                     live = jnp.logical_and(rows_ref[slot] == target, slot < count_ref[0])
                     term = products[slot] * jnp.where(live, 1.0, 0.0)
                     total = term if total is None else total + term
-                part[ch, target] = total
+                return total
 
             arrive = sums_z[step][ch]
 
@@ -219,10 +219,12 @@
                 )
 
             def mine_for(k):
-                return part[ch, wrap(z + k * s, NZ)]
-
-            fore = pass_on(0, mine_for(4), s)
-            back = pass_on(4, mine_for(-3), -s)
+                return part[ch, k % NZ]
+
+            fore = pass_on(0, partial_sum(4), s)
+            back = pass_on(4, partial_sum(-3), -s)
+            for k in (3, -2, 2, -1, 1, 0):
+                part[ch, k % NZ] = partial_sum(k)
             yield
             for k in range(1, 4):
                 fore.wait_recv()
@@ -232,7 +234,7 @@
                     back = pass_on(4 + k, mine_for(k - 3) + arrive[3 + k].astype(jnp.float32), -s)
                 yield
             back.wait_recv()
-            raw = part[ch, z] + arrive[6].astype(jnp.float32)
+            raw = part[ch, 0] + arrive[6].astype(jnp.float32)
             fore.wait_recv()
             raw = raw + arrive[3].astype(jnp.float32)
 
@@ -245,7 +247,7 @@
                 v0 = vec[0, qs, :] * inv
                 vec[0, qs, :] = v0
                 act[0, qs, :] = image
-                dots = [dot(v0, image), dot(image, image), dot(v0, v0)]
+                pending = [(v0, image), (image, image), (v0, v0)]
             elif step == 1:
                 va, aa, vv = g[0:1], g[1:2], g[2:3]
                 h00 = va + d * vv
@@ -261,7 +263,7 @@
                 image = (raw + e_col * a0) * h_col
                 vec[1, qs, :] = v1
                 act[1, qs, :] = image
-                dots = [dot(v0, image), dot(v1, image), dot(image, image), dot(v0, v1), dot(v1, v1)]
+                pending = [(v0, image), (v1, image), (image, image), (v0, v1), (v1, v1)]
             else:
                 va0, va1, aa, v01, v11 = (g[k : k + 1] for k in range(5))
                 v00 = known["vv00"]
@@ -283,13 +285,12 @@
                 v2 = (a1 + e_col * v1 - f_col * v0) * h_col
                 image = (raw + e_col * a1 - f_col * a0) * h_col
                 vec[2, qs, :] = v2
-                dots = [
-                    dot(v0, image), dot(v1, image), dot(v2, image), dot(image, image),
-                    dot(v0, v2), dot(v1, v2), dot(v2, v2),
+                pending = [
+                    (v0, image), (v1, image), (v2, image), (image, image), (v0, v2), (v1, v2), (v2, v2)
                 ]
             if step + 1 < ITERS:
                 gathered[step + 1][ch][own] = image.astype(jnp.bfloat16)
-            shared["rows"].append(dots)
+        shared["rows"].append([dot(*both) for both in pending])
         yield
 
         g = shared["total"]
@@ -410,7 +411,8 @@
             pltpu.VMEM((8, QUERIES), f32),
             pltpu.VMEM((ITERS + 1, TILE, QUERIES), f32),
             pltpu.VMEM((ITERS + 1, ITERS, QUERIES), f32),
-            pltpu.VMEM((ITERS + 1, CHUNKS // GROUP, NZ * 2, 8, 128), f32),
+            pltpu.VMEM((ITERS + 1, CHUNKS // GROUP, NZ, 8, 128), f32),
+            pltpu.VMEM((ITERS + 1, CHUNKS // GROUP, 2, 8, 128), f32),
             pltpu.VMEM((ITERS + 1, CHUNKS // GROUP, NX * NY, 8, 128), f32),
             dma((2,)),
             dma((ITERS + 2,)),
@@ -418,8 +420,8 @@
             dma((ITERS, CHUNKS, 8)),
             dma((ITERS, CHUNKS, 7)),
             dma((ITERS, CHUNKS, 7)),
-            dma((ITERS + 1, CHUNKS // GROUP, 2)),
-            dma((ITERS + 1, CHUNKS // GROUP, 2)),
+            dma((ITERS + 1, CHUNKS // GROUP, 3)),
+            dma((ITERS + 1, CHUNKS // GROUP, 3)),
         ],
         compiler_params=pltpu.CompilerParams(
             collective_id=0, has_side_effects=True, vmem_limit_bytes=60 * 1024 * 1024

time: 118 us -> 117 us (level)
  no operation moved by 1% of the time
where the time goes in v4:
time: 117 us
  Pallas kernels  112 us (96%)
  local copies, waits for them, and re-layouts  3.55 us (3%)
  between operations  1.29 us (1%)
    pallas_call x1, Pallas kernels, on_device(): pl.pallas_call(functools.partial(kernel, rescale), out_shape=(jax.ShapeDt...  112 us

profile of v4, /device:TPU:1, one launch (start us, length us, event | category | flops | bytes accessed | tf_op | source)
XLA Modules:
  0.0 117.2 jit_solution(2619295230126753297)
XLA Ops:
  1.3 112.3 %shard_map.77 = (f32[4,512,128]{2,1,0:T(8,128)}, f32[4,3,128]{2,1,0:T(4,128)}) custom-call(s32[4]{0:T(128)} %bitcast.7, s32[4]{0:T(128)} %bitcast.8, s32[1]{0:T(128)} %bitcast.5.count_ref, f32[1,128]{1,0:T(1,128)} %bitcast.9, f32[512,128]{1,0:T(8,128)} %right_ref.1, bf16[4,512,512]{2,1,0:T(8,128)(2,1)} %bitcast.6), custom_call_target="tpu_custom_call" | custom-call | tf_op jit(solution)/shard_map/pallas_call | solution.py:393
  113.6 1.3 %copy.8 = f32[4,3,128]{2,0,1:T(4,128)} copy(f32[4,3,128]{2,1,0:T(4,128)} %get-tuple-element.3) | data formatting | bytes 12288 | tf_op jit(solution)/shard_map/pallas_call | solution.py:393
  114.9 2.3 %copy.11 = f32[4,512,128]{2,1,0:T(8,128)} copy(f32[4,512,128]{2,1,0:T(8,128)} %get-tuple-element.6) | data formatting | bytes 2097152

commit v5 on v4

--- a/solution.py
+++ b/solution.py
@@ -394,7 +394,7 @@
         functools.partial(kernel, rescale),
         out_shape=(
             jax.ShapeDtypeStruct((ITERS + 1, width, queries), f32),
-            jax.ShapeDtypeStruct((ITERS + 1, ITERS, queries), f32),
+            jax.ShapeDtypeStruct((ITERS + 1, 8, queries), f32),
         ),
         in_specs=[smem, smem, smem, vmem, hbm, hbm],
         out_specs=(hbm, hbm),
@@ -410,7 +410,7 @@
             pltpu.VMEM((ITERS, CHUNKS, 7, QC, TILE), bf16),
             pltpu.VMEM((8, QUERIES), f32),
             pltpu.VMEM((ITERS + 1, TILE, QUERIES), f32),
-            pltpu.VMEM((ITERS + 1, ITERS, QUERIES), f32),
+            pltpu.VMEM((ITERS + 1, 8, QUERIES), f32),
             pltpu.VMEM((ITERS + 1, CHUNKS // GROUP, NZ, 8, 128), f32),
             pltpu.VMEM((ITERS + 1, CHUNKS // GROUP, 2, 8, 128), f32),
             pltpu.VMEM((ITERS + 1, CHUNKS // GROUP, NX * NY, 8, 128), f32),
@@ -430,7 +430,7 @@
         tile_row.reshape(SLOTS), tile_col.reshape(SLOTS), tile_count.reshape(1),
         damping.reshape(1, queries), right_side, tiles.reshape(SLOTS, TILE, TILE),
     )
-    return basis, hessenberg
+    return basis, hessenberg[:, :ITERS]
 
 
 def solution(mesh):

time: 117 us -> 117 us (level)
    pallas_call x1 -> x0, local copies, waits for them, and re-layouts: 1.29 us -> none  [on_device(): pl.pallas_call(functools.partial(kernel, rescale), out_shape=(jax.ShapeDt...]
    unnamed x1 -> x2, local copies, waits for them, and re-layouts: 2.26 us -> 2.86 us
where the time goes in v5:
time: 117 us
  Pallas kernels  112 us (96%)
  local copies, waits for them, and re-layouts  3.58 us (3%)
  between operations  1.29 us (1%)
    pallas_call x1, Pallas kernels, on_device(): pl.pallas_call(functools.partial(kernel, rescale), out_shape=(jax.ShapeDt...  112 us
    unnamed x2, local copies, waits for them, and re-layouts  2.86 us

profile of v5, /device:TPU:1, one launch (start us, length us, event | category | flops | bytes accessed | tf_op | source)
XLA Modules:
  0.0 117.2 jit_solution(7220640921211176913)
XLA Ops:
  1.3 112.3 %shard_map.77 = (f32[4,512,128]{2,1,0:T(8,128)}, f32[4,8,128]{2,1,0:T(8,128)}) custom-call(s32[4]{0:T(128)} %bitcast.7, s32[4]{0:T(128)} %bitcast.8, s32[1]{0:T(128)} %bitcast.5.count_ref, f32[1,128]{1,0:T(1,128)} %bitcast.9, f32[512,128]{1,0:T(8,128)} %right_ref.1, bf16[4,512,512]{2,1,0:T(8,128)(2,1)} %bitcast.6), custom_call_target="tpu_custom_call" | custom-call | tf_op jit(solution)/shard_map/pallas_call | solution.py:393
  113.6 0.7 slice.3
  114.3 0.6 copy.8
  114.9 2.3 %copy.11 = f32[4,512,128]{2,1,0:T(8,128)} copy(f32[4,512,128]{2,1,0:T(8,128)} %get-tuple-element.10) | data formatting | bytes 2097152
